TPU v7x, 128 devices: a whole 4x4x4 slice. The times are simulated.
128 devices in a mesh: row: 16 (over z, y), col: 8 (over x, core).
Axes of the slice: x: 4, y: 4, z: 4, core: 2. Of those that a mesh axis runs over, the one named last changes fastest.
Arguments:
- features: float32 [65536, 512], P(('row', 'col')), may hold values from -6 to 6
- tiles: float32 [16, 8, 128, 128, 128], P('row', 'col'), may hold values from -0.4 to 0.4
- tile_rows: int32 [16, 8, 128], P('row', 'col'), may hold values from 0 to 31
- tile_cols: int32 [16, 8, 128], P('row', 'col'), may hold values from 0 to 31
- tile_count: int32 [16, 8], P('row', 'col'), may hold values from 16 to 128, as said below
- needed: int32 [16, 8, 16, 2], P('row', 'col'), may hold values from 0 to 3, as said below
- w_in: bfloat16 [512, 2048], replicated, may hold values from -0.25 to 0.25
- bias_in: float32 [2048], replicated, may hold values from -5 to 5
- w_out: bfloat16 [2048, 512], replicated, may hold values from -0.125 to 0.125
- bias_out: float32 [512], replicated, may hold values from -5 to 5
Outputs:
- updated: bfloat16 [65536, 512], P(('row', 'col'))
Inputs may be any that keep to these rules, and one draw needn't show every extreme that they name: tile_count of every grid cell lies between 16 and 64, except one cell of each draw that has all 128 tiles live. Each list needed[r, c, q] holds 2 different block numbers.
All inputs are finite; a program needn't handle non-finite values.
Results may differ from a plain program's by a relative error of at most 0.0054.
Values sent between devices are 32-bit elements; how exact they have to be, the bound alone decides.
No kernel may reach another device: no remote copies, remote signals or barrier semaphores. Data moves between devices by JAX's collectives and lax.ppermute only.
A program may use at most 128 MiB of HBM per device.

v0:
```python
import math
import jax
import jax.numpy as jnp
from jax import lax
from jax.sharding import PartitionSpec as P

gin_epsilon = 0.25
precise_mode = lax.Precision.HIGHEST


def on_device(
    features, tiles, tile_rows, tile_cols, tile_count, needed, w_in, bias_in, w_out, bias_out
):
    tile_edge = tiles.shape[-1]
    width = features.shape[1]
    blocks_dev = features.shape[0] // tile_edge
    grid_cols = lax.axis_size("col")
    slot_count = needed.shape[-1]
    own_blocks = features.reshape(blocks_dev, tile_edge, width)
    my_tiles = tiles[0, 0]
    tile_row = tile_rows[0, 0]
    tile_col = tile_cols[0, 0]
    wanted = needed[0, 0]
    column_pool = lax.all_gather(own_blocks, "row", axis=0, tiled=True)
    source = tile_col // slot_count
    position = source * blocks_dev + jnp.take(wanted.reshape(-1), tile_col)
    tile_total = my_tiles.shape[0]
    group = math.gcd(32, tile_total)
    row_blocks = grid_cols * blocks_dev
    live = (jnp.arange(tile_total) < tile_count[0, 0]).astype(jnp.float32)
    block_ids = jnp.arange(row_blocks, dtype=jnp.int32)

    def add_group(turn, partial_value):
        start = turn * group
        group_tiles = lax.dynamic_slice_in_dim(my_tiles, start, group, 0)
        group_pos = lax.dynamic_slice_in_dim(position, start, group, 0)
        group_row = lax.dynamic_slice_in_dim(tile_row, start, group, 0)
        group_live = lax.dynamic_slice_in_dim(live, start, group, 0)
        inputs = jnp.take(column_pool, group_pos, axis=0)
        product = jnp.einsum("tpq,tqf->tpf", group_tiles, inputs, precision=precise_mode)
        selector = (group_row[None, :] == block_ids[:, None]).astype(jnp.float32) * group_live[
            None, :
        ]
        return partial_value + jnp.dot(
            selector, product.reshape(group, tile_edge * width), precision=precise_mode
        )

    partial_value = lax.fori_loop(
        0, tile_total // group, add_group, jnp.zeros((row_blocks, tile_edge * width), jnp.float32)
    )
    summed = lax.psum_scatter(
        partial_value.reshape(row_blocks * tile_edge, width), "col", scatter_dimension=0, tiled=True
    )
    mixed = ((1.0 + gin_epsilon) * features + summed).astype(jnp.bfloat16)
    hidden = jax.nn.relu(jnp.dot(mixed, w_in, preferred_element_type=jnp.float32) + bias_in).astype(
        jnp.bfloat16
    )
    return (jnp.dot(hidden, w_out, preferred_element_type=jnp.float32) + bias_out).astype(
        jnp.bfloat16
    )


def solution(mesh):
    placed = (
        P(("row", "col"), None),
        P("row", "col", None, None, None),
        P("row", "col", None),
        P("row", "col", None),
        P("row", "col"),
        P("row", "col", None, None),
        P(),
        P(),
        P(),
        P(),
    )
    return jax.shard_map(
        on_device, mesh=mesh, in_specs=placed, out_specs=P(("row", "col"), None), check_vma=False
    )
```

profile of v0, /device:TPU:1, one launch (start us, length us, event | category | flops | bytes accessed | tf_op | source)
XLA Modules:
  0.0 363.8 jit_solution(9578048227056878667)
XLA Ops:
  6.5 0.0 copy-start
  6.5 0.0 all-gather.2.cloned.1.call-start
  6.5 0.7 all-gather.2.cloned.1.call-update
  7.3 0.0 reduce-scatter.2.cloned.1.call-start
  7.3 0.8 copy.13
  8.1 0.1 reshape_squeeze.3
  8.8 0.7 fusion.18
  9.5 1.2 gather_fusion.1
  10.7 0.7 fusion.17
  11.4 112.5 %all-gather.2.cloned.1.call-done = f32[64,128,512]{2,1,0:T(8,128)} async-done(((f32[4,128,512]{2,1,0:T(8,128)}), f32[64,128,512]{2,1,0:T(8,128)}) %all-gather.2.cloned.1.call-update) | async-done | bytes 16777232 | tf_op jit(solution)/shard_map/all_gather | solution.py:24
  123.9 168.7 %while.14 = (s32[]{:T(128)}, f32[32,65536]{1,0:T(8,128)}, s32[128]{0:T(128)}, f32[128]{0:T(128)S(1)}, f32[128,128,128]{2,1,0:T(8,128)}, /*index=5*/s32[128]{0:T(...) while((s32[]{:T(128)}, f32[32,65536]{1,0:T(8,128)}, ...), condition=%wide.region_1.2_spmd.clone, body=%wide.region_0.1_spmd.clone.sunk | while | flops 4032826624 | bytes 77602320 | solution.py:48
  123.9 0.1 compare_and_fusion.2
  124.0 10.1 %gather_fusion = f32[32,128,512]{2,1,0:T(8,128)} fusion(f32[64,128,512]{2,1,0:T(8,128)} %get-tuple-element.262, s32[1024]{0:T(1024)S(1)} %pad_clamp_fusion.3), kind=kCustom, calls=%fused_computation.clone.clone.1 | custom fusion | bytes 16777344 | tf_op jit(solution)/shard_map/while/body/eval_jaxpr/jit(_take)/gather | solution.py:39
  134.0 10.9 %fusion.34 = f32[32,128,512]{2,1,0:T(8,128)S(1)} fusion(f32[32,128,512]{2,1,0:T(8,128)} %gather_fusion, pred[32]{0:T(512)(128)(4,1)S(1)} %get-tuple-element.233, f32[128,128,128]{2,1,0:T(8,128)} %get-tuple-element.260, s32[]{:T(128)S(6)} %select_n.79), kind=kOutput, calls=%fused_computation.4.clone.1 | convolution fusion | flops 3223322624 | bytes 18874404 | tf_op jit(solution)/shard_map/while/body/eval_jaxpr/tpq,tqf->tpf/dot_general | solution.py:40
  145.0 0.0 copy-start.4
  145.0 8.1 %copy.16 = f32[4,8,128,512]{3,1,2,0:T(8,128)} copy(f32[4,8,128,512]{3,2,1,0:T(8,128)S(1)} %bitcast.33) | data formatting | bytes 16777216 | tf_op jit(solution)/shard_map/while
  153.1 0.1 dynamic_slice.40
  153.1 0.0 copy-done.4
  153.1 0.1 dynamic_slice.41
  153.2 11.9 %convolution_add_fusion.3 = f32[32,65536]{1,0:T(8,128)} fusion(f32[32,65536]{1,0:T(8,128)} %bitcast.34, f32[32,65536]{1,0:T(8,128)} %get-tuple-element.246, pred[]{:T(512)S(6)} %compare.5, f32[32]{0:T(128)S(1)} %dynamic_slice.40, s32[32]{0:T(128)S(1)} %dynamic_slice.41), kind=kOutput, calls=%fused_computation.3.clone.1 | convolution fusion | flops 809502720 | bytes 25166080 | tf_op jit(solution)/shard_map/while/body/eval_jaxpr/dot_general | solution.py:44
  165.1 0.1 compare_and_fusion.2
  165.2 10.1 %gather_fusion = f32[32,128,512]{2,1,0:T(8,128)} fusion(f32[64,128,512]{2,1,0:T(8,128)} %get-tuple-element.262, s32[1024]{0:T(1024)S(1)} %pad_clamp_fusion.3), kind=kCustom, calls=%fused_computation.clone.clone.1 | custom fusion | bytes 16777344 | tf_op jit(solution)/shard_map/while/body/eval_jaxpr/jit(_take)/gather | solution.py:39
  175.3 10.9 %fusion.34 = f32[32,128,512]{2,1,0:T(8,128)S(1)} fusion(f32[32,128,512]{2,1,0:T(8,128)} %gather_fusion, pred[32]{0:T(512)(128)(4,1)S(1)} %get-tuple-element.233, f32[128,128,128]{2,1,0:T(8,128)} %get-tuple-element.260, s32[]{:T(128)S(6)} %select_n.79), kind=kOutput, calls=%fused_computation.4.clone.1 | convolution fusion | flops 3223322624 | bytes 18874404 | tf_op jit(solution)/shard_map/while/body/eval_jaxpr/tpq,tqf->tpf/dot_general | solution.py:40
  186.2 0.0 copy-start.4
  186.2 8.1 %copy.16 = f32[4,8,128,512]{3,1,2,0:T(8,128)} copy(f32[4,8,128,512]{3,2,1,0:T(8,128)S(1)} %bitcast.33) | data formatting | bytes 16777216 | tf_op jit(solution)/shard_map/while
  194.3 0.1 dynamic_slice.40
  194.3 0.0 copy-done.4
  194.3 0.1 dynamic_slice.41
  194.4 13.2 %convolution_add_fusion.3 = f32[32,65536]{1,0:T(8,128)} fusion(f32[32,65536]{1,0:T(8,128)} %bitcast.34, f32[32,65536]{1,0:T(8,128)} %get-tuple-element.246, pred[]{:T(512)S(6)} %compare.5, f32[32]{0:T(128)S(1)} %dynamic_slice.40, s32[32]{0:T(128)S(1)} %dynamic_slice.41), kind=kOutput, calls=%fused_computation.3.clone.1 | convolution fusion | flops 809502720 | bytes 25166080 | tf_op jit(solution)/shard_map/while/body/eval_jaxpr/dot_general | solution.py:44
  207.6 0.1 compare_and_fusion.2
  207.7 10.1 %gather_fusion = f32[32,128,512]{2,1,0:T(8,128)} fusion(f32[64,128,512]{2,1,0:T(8,128)} %get-tuple-element.262, s32[1024]{0:T(1024)S(1)} %pad_clamp_fusion.3), kind=kCustom, calls=%fused_computation.clone.clone.1 | custom fusion | bytes 16777344 | tf_op jit(solution)/shard_map/while/body/eval_jaxpr/jit(_take)/gather | solution.py:39
  217.8 10.9 %fusion.34 = f32[32,128,512]{2,1,0:T(8,128)S(1)} fusion(f32[32,128,512]{2,1,0:T(8,128)} %gather_fusion, pred[32]{0:T(512)(128)(4,1)S(1)} %get-tuple-element.233, f32[128,128,128]{2,1,0:T(8,128)} %get-tuple-element.260, s32[]{:T(128)S(6)} %select_n.79), kind=kOutput, calls=%fused_computation.4.clone.1 | convolution fusion | flops 3223322624 | bytes 18874404 | tf_op jit(solution)/shard_map/while/body/eval_jaxpr/tpq,tqf->tpf/dot_general | solution.py:40
  228.7 0.0 copy-start.4
  228.7 8.1 %copy.16 = f32[4,8,128,512]{3,1,2,0:T(8,128)} copy(f32[4,8,128,512]{3,2,1,0:T(8,128)S(1)} %bitcast.33) | data formatting | bytes 16777216 | tf_op jit(solution)/shard_map/while
  236.8 0.1 dynamic_slice.40
  236.8 0.0 copy-done.4
  236.8 0.1 dynamic_slice.41
  236.9 13.2 %convolution_add_fusion.3 = f32[32,65536]{1,0:T(8,128)} fusion(f32[32,65536]{1,0:T(8,128)} %bitcast.34, f32[32,65536]{1,0:T(8,128)} %get-tuple-element.246, pred[]{:T(512)S(6)} %compare.5, f32[32]{0:T(128)S(1)} %dynamic_slice.40, s32[32]{0:T(128)S(1)} %dynamic_slice.41), kind=kOutput, calls=%fused_computation.3.clone.1 | convolution fusion | flops 809502720 | bytes 25166080 | tf_op jit(solution)/shard_map/while/body/eval_jaxpr/dot_general | solution.py:44
  250.1 0.1 compare_and_fusion.2
  250.2 10.1 %gather_fusion = f32[32,128,512]{2,1,0:T(8,128)} fusion(f32[64,128,512]{2,1,0:T(8,128)} %get-tuple-element.262, s32[1024]{0:T(1024)S(1)} %pad_clamp_fusion.3), kind=kCustom, calls=%fused_computation.clone.clone.1 | custom fusion | bytes 16777344 | tf_op jit(solution)/shard_map/while/body/eval_jaxpr/jit(_take)/gather | solution.py:39
  260.2 10.9 %fusion.34 = f32[32,128,512]{2,1,0:T(8,128)S(1)} fusion(f32[32,128,512]{2,1,0:T(8,128)} %gather_fusion, pred[32]{0:T(512)(128)(4,1)S(1)} %get-tuple-element.233, f32[128,128,128]{2,1,0:T(8,128)} %get-tuple-element.260, s32[]{:T(128)S(6)} %select_n.79), kind=kOutput, calls=%fused_computation.4.clone.1 | convolution fusion | flops 3223322624 | bytes 18874404 | tf_op jit(solution)/shard_map/while/body/eval_jaxpr/tpq,tqf->tpf/dot_general | solution.py:40
  271.2 0.0 copy-start.4
  271.2 8.1 %copy.16 = f32[4,8,128,512]{3,1,2,0:T(8,128)} copy(f32[4,8,128,512]{3,2,1,0:T(8,128)S(1)} %bitcast.33) | data formatting | bytes 16777216 | tf_op jit(solution)/shard_map/while
  279.3 0.1 dynamic_slice.40
  279.3 0.0 copy-done.4
  279.3 0.1 dynamic_slice.41
  279.4 13.2 %convolution_add_fusion.3 = f32[32,65536]{1,0:T(8,128)} fusion(f32[32,65536]{1,0:T(8,128)} %bitcast.34, f32[32,65536]{1,0:T(8,128)} %get-tuple-element.246, pred[]{:T(512)S(6)} %compare.5, f32[32]{0:T(128)S(1)} %dynamic_slice.40, s32[32]{0:T(128)S(1)} %dynamic_slice.41), kind=kOutput, calls=%fused_computation.3.clone.1 | convolution fusion | flops 809502720 | bytes 25166080 | tf_op jit(solution)/shard_map/while/body/eval_jaxpr/dot_general | solution.py:44
  292.6 7.5 %reshape.58 = f32[4096,512]{1,0:T(8,128)} reshape(f32[32,65536]{1,0:T(8,128)} %get-tuple-element.144) | data formatting | bytes 16777216 | tf_op jit(solution)/shard_map/reshape | solution.py:52
  300.1 0.0 copy-start.1
  300.1 0.0 copy-start.2
  300.1 0.0 copy-start.3
  300.1 0.0 reduce-scatter.2.cloned.1.call-update
  300.1 51.8 %reduce-scatter.2.cloned.1.call-done = f32[512,512]{1,0:T(8,128)} async-done(((f32[4096,512]{1,0:T(8,128)}), f32[512,512]{1,0:T(8,128)}) %reduce-scatter.2.cloned.1.call-update) | async-done | bytes 1048592 | tf_op jit(solution)/shard_map/reduce_scatter | solution.py:51
  351.9 0.0 copy-done
  351.9 0.0 copy-done.1
  351.9 0.0 copy-done.2
  351.9 0.0 copy-done.3
  351.9 5.1 %fusion.14 = bf16[512,512]{1,0:T(8,128)(2,1)} fusion(bf16[2048,512]{1,0:T(8,128)(2,1)S(1)} %copy-done, bf16[512,2048]{1,0:T(8,128)(2,1)} %param.18, f32[2048]{0:T(1024)S(1)} %copy-done.2, f32[512,512]{1,0:T(8,128)} %reduce-scatter.2.cloned.1.call-done, f32[512,512]{1,0:T(8,128)S(1)} %copy-done.1, f32[512]{0:T(512)S(1)} %copy-done.3), kind=kOutput, calls=%fused_computation.22 | convolution fusion | flops 2151940096 | bytes 6825984 | tf_op jit(solution)/shard_map/dot_general | solution.py:58
  (7 shorter events, 0.0 us)
Async XLA Ops:
  6.5 345.4 %copy-start = (bf16[2048,512]{1,0:T(8,128)(2,1)S(1)}, bf16[2048,512]{1,0:T(8,128)(2,1)}, u32[]{:S(2)}) copy-start(bf16[2048,512]{1,0:T(8,128)(2,1)} %param.20) | copy-start | bytes 6291460
  6.5 117.3 %all-gather.2.cloned.1.call-start = ((), (), s32[]{:S(2)}) async-start(), calls=%async_computation.1 | async-start | bytes 17825792 | tf_op jit(solution)/shard_map/all_gather | solution.py:24
  7.3 344.6 %reduce-scatter.2.cloned.1.call-start = ((), (), s32[]{:S(2)}) async-start(), calls=%async_computation.2 | async-start | bytes 9437184 | tf_op jit(solution)/shard_map/reduce_scatter | solution.py:51
  145.0 8.2 %copy-start.4 = (s32[128]{0:T(128)S(1)}, s32[128]{0:T(128)}, u32[]{:S(2)}) copy-start(s32[128]{0:T(128)} %get-tuple-element.258) | copy-start | bytes 1540 | tf_op jit(solution)/shard_map/while
  186.2 8.2 %copy-start.4 = (s32[128]{0:T(128)S(1)}, s32[128]{0:T(128)}, u32[]{:S(2)}) copy-start(s32[128]{0:T(128)} %get-tuple-element.258) | copy-start | bytes 1540 | tf_op jit(solution)/shard_map/while
  228.7 8.2 %copy-start.4 = (s32[128]{0:T(128)S(1)}, s32[128]{0:T(128)}, u32[]{:S(2)}) copy-start(s32[128]{0:T(128)} %get-tuple-element.258) | copy-start | bytes 1540 | tf_op jit(solution)/shard_map/while
  271.2 8.2 %copy-start.4 = (s32[128]{0:T(128)S(1)}, s32[128]{0:T(128)}, u32[]{:S(2)}) copy-start(s32[128]{0:T(128)} %get-tuple-element.258) | copy-start | bytes 1540 | tf_op jit(solution)/shard_map/while
  300.1 51.8 %copy-start.1 = (f32[512,512]{1,0:T(8,128)S(1)}, f32[512,512]{1,0:T(8,128)}, u32[]{:S(2)}) copy-start(f32[512,512]{1,0:T(8,128)} %param.12) | copy-start | bytes 3145732
  300.1 51.8 %copy-start.2 = (f32[2048]{0:T(1024)S(1)}, f32[2048]{0:T(1024)}, u32[]{:S(2)}) copy-start(f32[2048]{0:T(1024)} %param.19) | copy-start | bytes 24580
  300.1 51.8 %copy-start.3 = (f32[512]{0:T(512)S(1)}, f32[512]{0:T(512)}, u32[]{:S(2)}) copy-start(f32[512]{0:T(512)} %param.21) | copy-start | bytes 6148
Sparse Core Ops, SparseCore 0:
  9.5 114.3 all-gather.1
  300.2 51.6 reduce-scatter.1
where the time goes:
time: 364 us
  waiting for transfers between devices  165 us (45%)
  matrix products  100 us (27%)
  local copies, waits for them, and re-layouts  82.8 us (23%)
  between operations  14.1 us (4%)
    all_gather x1, waiting for transfers between devices, on_device(): column_pool = lax.all_gather(own_blocks, 'row', axis=0, tiled=True)  112 us
    reduce_scatter x1, waiting for transfers between devices, on_device(): lax.psum_scatter(partial_value.reshape(row_blocks * tile_edge, width), 'c...  51.8 us
    dot_general x4, matrix products, add_group(): jnp.dot(selector, product.reshape(group, tile_edge * width), precision=pr...  51.4 us
    dot_general x4, matrix products, add_group(): jnp.einsum('tpq,tqf->tpf', group_tiles, inputs, precision=precise_mode)  43.6 us
    gather x4, local copies, waits for them, and re-layouts, add_group(): inputs = jnp.take(column_pool, group_pos, axis=0)  40.3 us
    while x12, local copies, waits for them, and re-layouts  32.4 us
    reshape x1, local copies, waits for them, and re-layouts, on_device(): partial_value.reshape(row_blocks * tile_edge, width)  7.49 us
  transfers between devices with their start and end apart: 2, of which 2 were waited for; matrix products, arithmetic and copies ran while one was open for 1% of the time, Pallas kernels for 0%

commit v1 on v0

--- a/solution.py
+++ b/solution.py
@@ -21,7 +21,9 @@
     tile_row = tile_rows[0, 0]
     tile_col = tile_cols[0, 0]
     wanted = needed[0, 0]
-    column_pool = lax.all_gather(own_blocks, "row", axis=0, tiled=True)
+    column_pool = jnp.concatenate(
+        lax.all_to_all(jnp.stack([own_blocks] * lax.axis_size("row")), "row", 0, 0), axis=0
+    )
     source = tile_col // slot_count
     position = source * blocks_dev + jnp.take(wanted.reshape(-1), tile_col)
     tile_total = my_tiles.shape[0]

time: 364 us -> 513 us (1.41)
  waiting for transfers between devices: 165 us -> 298 us
  starting transfers between devices: 0.04 us -> 8.81 us
  local copies, waits for them, and re-layouts: 82.8 us -> 91.3 us
    all_to_all x0 -> x1, waiting for transfers between devices: none -> 247 us  [on_device(): lax.all_to_all(jnp.stack([own_blocks] * lax.axis_size('row')), 'row', 0, 0)]
    all_gather x1 -> x0, waiting for transfers between devices: 112 us -> none  [on_device(): column_pool = lax.all_gather(own_blocks, 'row', axis=0, tiled=True)]
    another operation x0 -> x1, local copies, waits for them, and re-layouts: none -> 9.26 us  [on_device(): jnp.stack([own_blocks] * lax.axis_size('row'))]
    all_to_all x0 -> x1, starting transfers between devices: none -> 8.77 us  [on_device(): lax.all_to_all(jnp.stack([own_blocks] * lax.axis_size('row')), 'row', 0, 0)]
    while x12 -> x4, local copies, waits for them, and re-layouts: 32.4 us -> 32.3 us
  transfers between devices with their start and end apart: 2 -> 2, of which waited for: 2 -> 2; matrix products, arithmetic and copies ran while one was open for 1% -> 0% of each run, Pallas kernels for 0% -> 0%
where the time goes in v1:
time: 513 us; the launch traced here: 512 us
  waiting for transfers between devices  298 us (58%)
  matrix products  99.9 us (19%)
  local copies, waits for them, and re-layouts  91.3 us (18%)
  between operations  14.1 us (3%)
  starting transfers between devices  8.81 us (2%)
    all_to_all x1, waiting for transfers between devices, on_device(): lax.all_to_all(jnp.stack([own_blocks] * lax.axis_size('row')), 'row', 0, 0)  247 us
    dot_general x4, matrix products, add_group(): jnp.dot(selector, product.reshape(group, tile_edge * width), precision=pr...  51.2 us
    reduce_scatter x1, waiting for transfers between devices, on_device(): lax.psum_scatter(partial_value.reshape(row_blocks * tile_edge, width), 'c...  50.8 us
    dot_general x4, matrix products, add_group(): jnp.einsum('tpq,tqf->tpf', group_tiles, inputs, precision=precise_mode)  43.6 us
    gather x4, local copies, waits for them, and re-layouts, add_group(): inputs = jnp.take(column_pool, group_pos, axis=0)  40.3 us
    while x4, local copies, waits for them, and re-layouts  32.3 us
  transfers between devices with their start and end apart: 2, of which 2 were waited for; matrix products, arithmetic and copies ran while one was open for 0% of the time, Pallas kernels for 0%

profile of v1, /device:TPU:1, one launch (start us, length us, event | category | flops | bytes accessed | tf_op | source)
XLA Modules:
  0.0 512.3 jit_solution(9515069803146729856)
XLA Ops:
  6.5 0.0 copy-start
  6.5 9.3 %stack.3 = f32[16,4,128,512]{3,2,1,0:T(8,128)} broadcast(f32[4,128,512]{2,1,0:T(8,128)} %bitcast.37), dimensions={1,2,3} | broadcast | bytes 17825792 | tf_op jit(solution)/shard_map/stack | solution.py:25
  15.8 0.0 copy-start.2
  15.8 0.0 copy-start.5
  15.8 0.0 copy-start.6
  15.8 8.8 %all-to-all-start = ((f32[16,4,128,512]{3,2,1,0:T(8,128)}), f32[16,4,128,512]{3,2,1,0:T(8,128)}, u32[]{:S(2)}, u32[]{:S(2)}) async-start(f32[16,4,128,512]{3,2,1,0:T(8,128)} %stack.3), calls=%async_computation | async-start | bytes 33554432 | tf_op jit(solution)/shard_map/all_to_all | solution.py:25
  24.6 0.0 reduce-scatter.2.cloned.1.call-start
  24.6 0.0 copy-done.2
  24.7 0.1 copy.12
  24.7 0.1 reshape_squeeze.3
  25.5 0.0 copy-done.5
  25.5 1.2 gather_fusion.1
  26.8 246.9 %all-to-all-done = f32[16,4,128,512]{3,2,1,0:T(8,128)} async-done(((f32[16,4,128,512]{3,2,1,0:T(8,128)}), f32[16,4,128,512]{3,2,1,0:T(8,128)}, u32[]{:S(2)}, u32[]{:S(2)}) %all-to-all-start) | async-done | bytes 16777248 | tf_op jit(solution)/shard_map/all_to_all | solution.py:25
  273.7 0.0 copy-done.6
  273.7 168.3 %while.14 = (s32[]{:T(128)}, f32[32,65536]{1,0:T(8,128)}, s32[128]{0:T(128)S(1)}, f32[128]{0:T(128)S(1)}, f32[128,128,128]{2,1,0:T(8,128)}, /*index=5*/s32[128]{...) while((s32[]{:T(128)}, f32[32,65536]{1,0:T(8,128)}, ...), condition=%wide.region_1.2_spmd.clone, body=%wide.region_0.1_spmd.clone.sunk | while | flops 4032826624 | bytes 77600240 | solution.py:50
  273.7 0.1 compare_and_fusion.2
  273.8 10.1 %gather_fusion = f32[32,128,512]{2,1,0:T(8,128)} fusion(f32[64,128,512]{2,1,0:T(8,128)} %get-tuple-element.262, s32[1024]{0:T(1024)S(1)} %pad_clamp_fusion.3), kind=kCustom, calls=%fused_computation.clone.clone.1 | custom fusion | bytes 16777344 | tf_op jit(solution)/shard_map/while/body/eval_jaxpr/jit(_take)/gather | solution.py:41
  283.9 10.9 %fusion.34 = f32[32,128,512]{2,1,0:T(8,128)S(1)} fusion(f32[32,128,512]{2,1,0:T(8,128)} %gather_fusion, pred[32]{0:T(512)(128)(4,1)S(1)} %get-tuple-element.233, f32[128,128,128]{2,1,0:T(8,128)} %get-tuple-element.260, s32[]{:T(128)S(6)} %select_n.79), kind=kOutput, calls=%fused_computation.4.clone.1 | convolution fusion | flops 3223322624 | bytes 18874404 | tf_op jit(solution)/shard_map/while/body/eval_jaxpr/tpq,tqf->tpf/dot_general | solution.py:42
  294.8 8.1 %copy.15 = f32[4,8,128,512]{3,1,2,0:T(8,128)} copy(f32[4,8,128,512]{3,2,1,0:T(8,128)S(1)} %bitcast.34) | data formatting | bytes 16777216 | tf_op jit(solution)/shard_map/while
  302.9 0.1 dynamic_slice.40
  302.9 0.1 dynamic_slice.41
  303.0 11.8 %convolution_add_fusion.3 = f32[32,65536]{1,0:T(8,128)} fusion(f32[32,65536]{1,0:T(8,128)} %bitcast.35, f32[32,65536]{1,0:T(8,128)} %get-tuple-element.246, pred[]{:T(512)S(6)} %compare.5, f32[32]{0:T(128)S(1)} %dynamic_slice.40, s32[32]{0:T(128)S(1)} %dynamic_slice.41), kind=kOutput, calls=%fused_computation.3.clone.1 | convolution fusion | flops 809502720 | bytes 25166080 | tf_op jit(solution)/shard_map/while/body/eval_jaxpr/dot_general | solution.py:46
  314.8 0.1 compare_and_fusion.2
  314.9 10.1 %gather_fusion = f32[32,128,512]{2,1,0:T(8,128)} fusion(f32[64,128,512]{2,1,0:T(8,128)} %get-tuple-element.262, s32[1024]{0:T(1024)S(1)} %pad_clamp_fusion.3), kind=kCustom, calls=%fused_computation.clone.clone.1 | custom fusion | bytes 16777344 | tf_op jit(solution)/shard_map/while/body/eval_jaxpr/jit(_take)/gather | solution.py:41
  325.0 10.9 %fusion.34 = f32[32,128,512]{2,1,0:T(8,128)S(1)} fusion(f32[32,128,512]{2,1,0:T(8,128)} %gather_fusion, pred[32]{0:T(512)(128)(4,1)S(1)} %get-tuple-element.233, f32[128,128,128]{2,1,0:T(8,128)} %get-tuple-element.260, s32[]{:T(128)S(6)} %select_n.79), kind=kOutput, calls=%fused_computation.4.clone.1 | convolution fusion | flops 3223322624 | bytes 18874404 | tf_op jit(solution)/shard_map/while/body/eval_jaxpr/tpq,tqf->tpf/dot_general | solution.py:42
  335.9 8.1 %copy.15 = f32[4,8,128,512]{3,1,2,0:T(8,128)} copy(f32[4,8,128,512]{3,2,1,0:T(8,128)S(1)} %bitcast.34) | data formatting | bytes 16777216 | tf_op jit(solution)/shard_map/while
  344.0 0.1 dynamic_slice.40
  344.1 0.1 dynamic_slice.41
  344.1 13.1 %convolution_add_fusion.3 = f32[32,65536]{1,0:T(8,128)} fusion(f32[32,65536]{1,0:T(8,128)} %bitcast.35, f32[32,65536]{1,0:T(8,128)} %get-tuple-element.246, pred[]{:T(512)S(6)} %compare.5, f32[32]{0:T(128)S(1)} %dynamic_slice.40, s32[32]{0:T(128)S(1)} %dynamic_slice.41), kind=kOutput, calls=%fused_computation.3.clone.1 | convolution fusion | flops 809502720 | bytes 25166080 | tf_op jit(solution)/shard_map/while/body/eval_jaxpr/dot_general | solution.py:46
  357.2 0.1 compare_and_fusion.2
  357.3 10.1 %gather_fusion = f32[32,128,512]{2,1,0:T(8,128)} fusion(f32[64,128,512]{2,1,0:T(8,128)} %get-tuple-element.262, s32[1024]{0:T(1024)S(1)} %pad_clamp_fusion.3), kind=kCustom, calls=%fused_computation.clone.clone.1 | custom fusion | bytes 16777344 | tf_op jit(solution)/shard_map/while/body/eval_jaxpr/jit(_take)/gather | solution.py:41
  367.4 10.9 %fusion.34 = f32[32,128,512]{2,1,0:T(8,128)S(1)} fusion(f32[32,128,512]{2,1,0:T(8,128)} %gather_fusion, pred[32]{0:T(512)(128)(4,1)S(1)} %get-tuple-element.233, f32[128,128,128]{2,1,0:T(8,128)} %get-tuple-element.260, s32[]{:T(128)S(6)} %select_n.79), kind=kOutput, calls=%fused_computation.4.clone.1 | convolution fusion | flops 3223322624 | bytes 18874404 | tf_op jit(solution)/shard_map/while/body/eval_jaxpr/tpq,tqf->tpf/dot_general | solution.py:42
  378.3 8.1 %copy.15 = f32[4,8,128,512]{3,1,2,0:T(8,128)} copy(f32[4,8,128,512]{3,2,1,0:T(8,128)S(1)} %bitcast.34) | data formatting | bytes 16777216 | tf_op jit(solution)/shard_map/while
  386.4 0.1 dynamic_slice.40
  386.5 0.1 dynamic_slice.41
  386.5 13.1 %convolution_add_fusion.3 = f32[32,65536]{1,0:T(8,128)} fusion(f32[32,65536]{1,0:T(8,128)} %bitcast.35, f32[32,65536]{1,0:T(8,128)} %get-tuple-element.246, pred[]{:T(512)S(6)} %compare.5, f32[32]{0:T(128)S(1)} %dynamic_slice.40, s32[32]{0:T(128)S(1)} %dynamic_slice.41), kind=kOutput, calls=%fused_computation.3.clone.1 | convolution fusion | flops 809502720 | bytes 25166080 | tf_op jit(solution)/shard_map/while/body/eval_jaxpr/dot_general | solution.py:46
  399.6 0.1 compare_and_fusion.2
  399.7 10.1 %gather_fusion = f32[32,128,512]{2,1,0:T(8,128)} fusion(f32[64,128,512]{2,1,0:T(8,128)} %get-tuple-element.262, s32[1024]{0:T(1024)S(1)} %pad_clamp_fusion.3), kind=kCustom, calls=%fused_computation.clone.clone.1 | custom fusion | bytes 16777344 | tf_op jit(solution)/shard_map/while/body/eval_jaxpr/jit(_take)/gather | solution.py:41
  409.8 10.9 %fusion.34 = f32[32,128,512]{2,1,0:T(8,128)S(1)} fusion(f32[32,128,512]{2,1,0:T(8,128)} %gather_fusion, pred[32]{0:T(512)(128)(4,1)S(1)} %get-tuple-element.233, f32[128,128,128]{2,1,0:T(8,128)} %get-tuple-element.260, s32[]{:T(128)S(6)} %select_n.79), kind=kOutput, calls=%fused_computation.4.clone.1 | convolution fusion | flops 3223322624 | bytes 18874404 | tf_op jit(solution)/shard_map/while/body/eval_jaxpr/tpq,tqf->tpf/dot_general | solution.py:42
  420.7 8.1 %copy.15 = f32[4,8,128,512]{3,1,2,0:T(8,128)} copy(f32[4,8,128,512]{3,2,1,0:T(8,128)S(1)} %bitcast.34) | data formatting | bytes 16777216 | tf_op jit(solution)/shard_map/while
  428.8 0.1 dynamic_slice.40
  428.9 0.1 dynamic_slice.41
  428.9 13.1 %convolution_add_fusion.3 = f32[32,65536]{1,0:T(8,128)} fusion(f32[32,65536]{1,0:T(8,128)} %bitcast.35, f32[32,65536]{1,0:T(8,128)} %get-tuple-element.246, pred[]{:T(512)S(6)} %compare.5, f32[32]{0:T(128)S(1)} %dynamic_slice.40, s32[32]{0:T(128)S(1)} %dynamic_slice.41), kind=kOutput, calls=%fused_computation.3.clone.1 | convolution fusion | flops 809502720 | bytes 25166080 | tf_op jit(solution)/shard_map/while/body/eval_jaxpr/dot_general | solution.py:46
  442.1 7.5 %reshape.60 = f32[4096,512]{1,0:T(8,128)} reshape(f32[32,65536]{1,0:T(8,128)} %get-tuple-element.144) | data formatting | bytes 16777216 | tf_op jit(solution)/shard_map/reshape | solution.py:54
  449.5 0.0 copy-start.1
  449.5 0.0 copy-start.3
  449.5 0.0 copy-start.4
  449.5 0.0 reduce-scatter.2.cloned.1.call-update
  449.6 50.8 %reduce-scatter.2.cloned.1.call-done = f32[512,512]{1,0:T(8,128)} async-done(((f32[4096,512]{1,0:T(8,128)}), f32[512,512]{1,0:T(8,128)}) %reduce-scatter.2.cloned.1.call-update) | async-done | bytes 1048592 | tf_op jit(solution)/shard_map/reduce_scatter | solution.py:53
  500.4 0.0 copy-done
  500.4 0.0 copy-done.1
  500.4 0.0 copy-done.3
  500.4 0.0 copy-done.4
  500.4 5.1 fusion.14
  (9 shorter events, 0.0 us)
Async XLA Ops:
  6.5 493.9 %copy-start = (bf16[2048,512]{1,0:T(8,128)(2,1)S(1)}, bf16[2048,512]{1,0:T(8,128)(2,1)}, u32[]{:S(2)}) copy-start(bf16[2048,512]{1,0:T(8,128)(2,1)} %param.20) | copy-start | bytes 6291460
  15.8 8.8 %copy-start.2 = (s32[1,1,16,2]{2,3,1,0:T(2,128)S(1)}, s32[1,1,16,2]{2,3,1,0:T(2,128)}, u32[]{:S(2)}) copy-start(s32[1,1,16,2]{2,3,1,0:T(2,128)} %param.17) | copy-start | bytes 388
  15.8 9.7 %copy-start.5 = (s32[1,1,128]{2,1,0:T(1,128)S(1)}, s32[1,1,128]{2,1,0:T(1,128)}, u32[]{:S(2)}) copy-start(s32[1,1,128]{2,1,0:T(1,128)} %param.15) | copy-start | bytes 1540
  15.8 257.9 %copy-start.6 = (s32[1,1,128]{2,1,0:T(1,128)S(1)}, s32[1,1,128]{2,1,0:T(1,128)}, u32[]{:S(2)}) copy-start(s32[1,1,128]{2,1,0:T(1,128)} %param.14) | copy-start | bytes 1540
  15.8 257.9 %all-to-all-start = ((f32[16,4,128,512]{3,2,1,0:T(8,128)}), f32[16,4,128,512]{3,2,1,0:T(8,128)}, u32[]{:S(2)}, u32[]{:S(2)}) async-start(f32[16,4,128,512]{3,2,1,0:T(8,128)} %stack.3), calls=%async_computation | async-start | bytes 33554432 | tf_op jit(solution)/shard_map/all_to_all | solution.py:25
  24.6 475.8 %reduce-scatter.2.cloned.1.call-start = ((), (), s32[]{:S(2)}) async-start(), calls=%async_computation.2 | async-start | bytes 9437184 | tf_op jit(solution)/shard_map/reduce_scatter | solution.py:53
  449.5 50.9 %copy-start.1 = (f32[512,512]{1,0:T(8,128)S(1)}, f32[512,512]{1,0:T(8,128)}, u32[]{:S(2)}) copy-start(f32[512,512]{1,0:T(8,128)} %param.12) | copy-start | bytes 3145732
  449.5 50.9 %copy-start.3 = (f32[2048]{0:T(1024)S(1)}, f32[2048]{0:T(1024)}, u32[]{:S(2)}) copy-start(f32[2048]{0:T(1024)} %param.19) | copy-start | bytes 24580
  449.5 50.9 %copy-start.4 = (f32[512]{0:T(512)S(1)}, f32[512]{0:T(512)}, u32[]{:S(2)}) copy-start(f32[512]{0:T(512)} %param.21) | copy-start | bytes 6148
Sparse Core Ops, SparseCore 0:
  449.7 50.6 reduce-scatter.1
